TPU v7x, 32 devices: a whole 2x2x4 slice. The times are simulated.
32 devices in a mesh: kz: 4 (over x, core), en: 8 (over z, y).
Axes of the slice: x: 2, y: 2, z: 4, core: 2. Of those that a mesh axis runs over, the one named last changes fastest.
Arguments:
- green_blocks: float32 [4, 16, 2, 256, 256], P('kz', 'en'), may hold values from -6 to 6
- couplings: float32 [4, 8, 2, 256, 256], P('kz', 'en'), may hold values from -0.375 to 0.375
- owners: int32 [2], replicated, may hold values from 0 to 31
- momentum_shift: int32 [2], replicated, may hold values from -3 to 3
- energy_shift: int32 [2], replicated, may hold values from 1 to 7
Outputs:
- self_energy: float32 [4, 16, 2, 256, 256], P('kz', 'en')
Inputs may be any that keep to these rules, and one draw needn't show every extreme that they name: `owners`: flat device index of each mode's coupling block.
All inputs are finite; a program needn't handle non-finite values.
Results may differ from a plain program's by a relative error of at most 0.0001.
Values sent between devices are 32-bit elements; how exact they have to be, the bound alone decides.
No kernel may reach another device: no remote copies, remote signals or barrier semaphores. Data moves between devices by JAX's collectives and lax.ppermute only.
A program may use at most 64 MiB of HBM per device.

v0:
```python
import jax
import jax.numpy as jnp
from jax import lax
from jax.sharding import PartitionSpec as P


def spread(array, axis, root):
    mine = lax.axis_index(axis) == root
    return lax.psum(jnp.where(mine, array, jnp.zeros_like(array)), axis)


def passed_along(block, axis, distance):
    devices = range(lax.axis_size(axis))
    route = [(i - distance, i) for i in devices if i - distance in devices]
    return lax.ppermute(block, axis, route)


def shifted(array, axis, by):
    devices = lax.axis_size(axis)
    return lax.ppermute(array, axis, [(i, (i + by) % devices) for i in range(devices)])


def matmul_left(left, right):
    return jnp.einsum("ij,...jk->...ik", left, right, precision=lax.Precision.HIGHEST)


def matmul_right(left, right):
    return jnp.einsum("...ij,kj->...ik", left, right, precision=lax.Precision.HIGHEST)


def sandwich(coupling, blocks):
    couple_real = coupling[0]
    couple_imag = coupling[1]
    green_real = blocks[..., 0, :, :]
    green_imag = blocks[..., 1, :, :]
    left_real = matmul_left(couple_real, green_real) - matmul_left(couple_imag, green_imag)
    left_imag = matmul_left(couple_real, green_imag) + matmul_left(couple_imag, green_real)
    out_real = matmul_right(left_real, couple_real) + matmul_right(left_imag, couple_imag)
    out_imag = matmul_right(left_imag, couple_real) - matmul_right(left_real, couple_imag)
    return jnp.stack([out_real, out_imag], axis=-3)


def pick_energies(own_blocks, lower_blocks, shift_value):
    local_count = own_blocks.shape[1]
    joined = jnp.concatenate([lower_blocks, own_blocks], axis=1)
    start = local_count - shift_value
    return lax.dynamic_slice_in_dim(joined, start, local_count, 1)


def bit_set(shift_value, bit_index):
    return shift_value // (1 << bit_index) % 2 == 1


def shards(green_blocks, couplings, owners, momentum_shift, energy_shift):
    coupling_list = []
    for mode_index in range(2):
        coupling_list.append(spread(couplings[0, 0], ("kz", "en"), owners[mode_index]))
    momentum_count = lax.axis_size("kz")
    bit_count = (momentum_count - 1).bit_length()
    local_count = green_blocks.shape[1]
    momentum_first = jnp.mod(momentum_shift[0], momentum_count)
    momentum_second = jnp.mod(momentum_shift[1], momentum_count)
    lower_blocks = passed_along(green_blocks, "en", 1)
    first = pick_energies(green_blocks, lower_blocks, energy_shift[0] % local_count)
    second = pick_energies(green_blocks, lower_blocks, energy_shift[1] % local_count)
    steps_first = energy_shift[0] // local_count
    steps_second = energy_shift[1] // local_count
    for bit_index in range(2):
        moved = passed_along((first, second), "en", 1 << bit_index)
        first = jnp.where(bit_set(steps_first, bit_index), moved[0], first)
        second = jnp.where(bit_set(steps_second, bit_index), moved[1], second)
    for bit_index in range(bit_count):
        moved = shifted((first, second), "kz", 1 << bit_index)
        first = jnp.where(bit_set(momentum_first, bit_index), moved[0], first)
        second = jnp.where(bit_set(momentum_second, bit_index), moved[1], second)
    first_term = sandwich(coupling_list[0], first)
    second_term = sandwich(coupling_list[1], second)
    result = first_term
    result = result + second_term
    return result


def solution(mesh):
    in_specs = (P("kz", "en", None, None, None), P("kz", "en", None, None, None), P(), P(), P())
    out_specs = P("kz", "en", None, None, None)
    return jax.shard_map(shards, mesh=mesh, in_specs=in_specs, out_specs=out_specs, check_vma=False)
```

profile of v0, /device:TPU:0, one launch (start us, length us, event | category | flops | bytes accessed | tf_op | source)
XLA Modules:
  0.0 311.8 jit_solution(17990503644076765318)
XLA Ops:
  6.5 1.6 copy.6
  8.1 5.9 %collective-permute-start = (f32[1,2,2,256,256]{3,4,1,2,0:T(8,128)S(1)}, f32[1,2,2,256,256]{3,4,1,2,0:T(8,128)}, u32[]{:S(2)}, u32[]{:S(2)}) collective-permute-start(f32[1,2,2,256,256]{3,4,1,2,0:T(8,128)S(1)} %copy.6), channel_id=1, source_target_pairs={{0,1},{1,2},{2,3},{3,4},{4,5},{5,6},{6,7},{8,9},{9,10},{10,11},{11... | collective-permute-start | bytes 3145736 | tf_op jit(solution)/shard_map/ppermute | solution.py:15
  18.5 17.0 %collective-permute-done = f32[1,2,2,256,256]{3,4,1,2,0:T(8,128)} collective-permute-done((f32[1,2,2,256,256]{3,4,1,2,0:T(8,128)S(1)}, f32[1,2,2,256,256]{3,4,1,2,0:T(8,128)}, u32[]{:S(2)}, u32[]{:S(2)}) %collective-permute-start) | collective-permute-done | bytes 1048608 | tf_op jit(solution)/shard_map/ppermute | solution.py:15
  35.7 4.6 %collective-permute-start.5 = (f32[1,2,2,256,256]{3,4,1,2,0:T(8,128)S(1)}, f32[1,2,2,256,256]{3,4,1,2,0:T(8,128)S(1)}, u32[]{:S(2)}, u32[]{:S(2)}) collective-permute-start(f32[1,2,2,256,256]{3,4,1,2,0:T(8,128)S(1)} %get-tuple-element.7), channel_id=1, source_target_pairs={{0,1},{1,2},{2,3},{3,4},{4,5},{5,6},{6,7},{8,9},{9,10},{10,11},{11... | collective-permute-start | bytes 3145736 | tf_op jit(solution)/shard_map/ppermute | solution.py:15
  40.3 5.2 %collective-permute-start.1 = (f32[1,2,2,256,256]{3,4,1,2,0:T(8,128)S(1)}, f32[1,2,2,256,256]{3,4,1,2,0:T(8,128)}, u32[]{:S(2)}, u32[]{:S(2)}) collective-permute-start(f32[1,2,2,256,256]{3,4,1,2,0:T(8,128)S(1)} %get-tuple-element.8), channel_id=1, source_target_pairs={{0,1},{1,2},{2,3},{3,4},{4,5},{5,6},{6,7},{8,9},{9,10},{10,11},{11... | collective-permute-start | bytes 3145736 | tf_op jit(solution)/shard_map/ppermute | solution.py:15
  46.2 17.5 %collective-permute-done.5 = f32[1,2,2,256,256]{3,4,1,2,0:T(8,128)S(1)} collective-permute-done((f32[1,2,2,256,256]{3,4,1,2,0:T(8,128)S(1)}, f32[1,2,2,256,256]{3,4,1,2,0:T(8,128)S(1)}, u32[]{:S(2)}, u32[]{:S(2)}) %collective-permute-start.5) | collective-permute-done | bytes 1048608 | tf_op jit(solution)/shard_map/ppermute | solution.py:15
  63.7 1.1 broadcast_select_fusion
  64.8 7.2 %collective-permute-start.6 = (f32[1,2,2,256,256]{3,4,1,2,0:T(8,128)}, f32[1,2,2,256,256]{3,4,1,2,0:T(8,128)}, u32[]{:S(2)}, u32[]{:S(2)}) collective-permute-start(f32[1,2,2,256,256]{3,4,1,2,0:T(8,128)} %broadcast_select_fusion), channel_id=1, source_target_pairs={{0,2},{1,3},{2,4},{3,5},{4,6},{5,7},{8,10},{9,11},{10,12},{11,13},... | collective-permute-start | bytes 3145736 | tf_op jit(solution)/shard_map/ppermute | solution.py:15
  72.7 11.5 %collective-permute-done.1 = f32[1,2,2,256,256]{3,4,1,2,0:T(8,128)} collective-permute-done((f32[1,2,2,256,256]{3,4,1,2,0:T(8,128)S(1)}, f32[1,2,2,256,256]{3,4,1,2,0:T(8,128)}, u32[]{:S(2)}, u32[]{:S(2)}) %collective-permute-start.1) | collective-permute-done | bytes 1048608 | tf_op jit(solution)/shard_map/ppermute | solution.py:15
  84.2 1.4 broadcast_select_fusion.4
  85.6 9.3 %collective-permute-start.2 = (f32[1,2,2,256,256]{3,4,1,2,0:T(8,128)S(1)}, f32[1,2,2,256,256]{3,4,1,2,0:T(8,128)}, u32[]{:S(2)}, u32[]{:S(2)}) collective-permute-start(f32[1,2,2,256,256]{3,4,1,2,0:T(8,128)S(1)} %broadcast_select_fusion.4), channel_id=1, source_target_pairs={{0,2},{1,3},{2,4},{3,5},{4,6},{5,7},{8,10},{9,11},{10,12},{11,13},... | collective-permute-start | bytes 3145736 | tf_op jit(solution)/shard_map/ppermute | solution.py:15
  94.9 1.4 broadcast_select_fusion.1
  96.4 16.2 %collective-permute-done.2 = f32[1,2,2,256,256]{3,4,1,2,0:T(8,128)} collective-permute-done((f32[1,2,2,256,256]{3,4,1,2,0:T(8,128)S(1)}, f32[1,2,2,256,256]{3,4,1,2,0:T(8,128)}, u32[]{:S(2)}, u32[]{:S(2)}) %collective-permute-start.2) | collective-permute-done | bytes 1048608 | tf_op jit(solution)/shard_map/ppermute | solution.py:15
  112.6 1.4 broadcast_select_fusion.5
  116.8 1.4 broadcast_select_fusion.2
  118.2 1.6 collective-permute-start.8
  123.6 11.6 %collective-permute-done.3 = f32[1,2,2,256,256]{3,4,1,2,0:T(8,128)} collective-permute-done((f32[1,2,2,256,256]{3,4,1,2,0:T(8,128)S(1)}, f32[1,2,2,256,256]{3,4,1,2,0:T(8,128)}, u32[]{:S(2)}, u32[]{:S(2)}) %collective-permute-start.3) | collective-permute-done | bytes 1048608 | tf_op jit(solution)/shard_map/ppermute | solution.py:20
  135.3 1.6 collective-permute-start.4
  136.9 1.1 select_bitcast_fusion
  138.0 6.4 %collective-permute-done.8 = f32[1,2,2,256,256]{3,4,1,2,0:T(8,128)} collective-permute-done((f32[1,2,2,256,256]{3,4,1,2,0:T(8,128)S(1)}, f32[1,2,2,256,256]{3,4,1,2,0:T(8,128)}, u32[]{:S(2)}, u32[]{:S(2)}) %collective-permute-start.8) | collective-permute-done | bytes 1048608 | tf_op jit(solution)/shard_map/ppermute | solution.py:20
  144.4 1.4 broadcast_select_fusion.3
  145.8 142.2 %all-reduce.3.cloned.1.call-done = (f32[2,256,256]{2,1,0:T(8,128)}, f32[2,256,256]{2,1,0:T(8,128)}) async-done(((f32[2,256,256]{2,1,0:T(8,128)}, f32[2,256,256]{2,1,0:T(8,128)}), (f32[2,256,256]{2,1,0:T(8,128)}, f32[2,256,256]{2,1,0:T(8,128)})) %all-reduce.3.cloned.1.call-update) | async-done | bytes 1048592 | tf_op jit(solution)/shard_map/psum | solution.py:9
  288.0 1.6 fusion.13
  290.3 1.4 broadcast_select_fusion.7
  295.3 1.0 fusion.16
  296.3 1.0 fusion.1
  297.3 1.0 fusion
  299.0 1.0 fusion.15
  300.6 1.0 fusion.14
  301.7 1.0 fusion.5
  302.7 1.0 fusion.4
  303.9 1.0 copy.16
  (33 shorter events, 8.0 us)
Async XLA Ops:
  6.5 7.5 %copy-start.3 = (s32[2]{0:T(128)S(1)}, s32[2]{0:T(128)}, u32[]{:S(2)}) copy-start(s32[2]{0:T(128)} %param.9) | copy-start | bytes 28
  6.5 281.5 %all-reduce.3.cloned.1.call-start = ((), (), s32[]{:S(2)}) async-start(), calls=%async_computation | async-start | bytes 2097152 | tf_op jit(solution)/shard_map/psum | solution.py:9
  8.1 27.3 %collective-permute-start = (f32[1,2,2,256,256]{3,4,1,2,0:T(8,128)S(1)}, f32[1,2,2,256,256]{3,4,1,2,0:T(8,128)}, u32[]{:S(2)}, u32[]{:S(2)}) collective-permute-start(f32[1,2,2,256,256]{3,4,1,2,0:T(8,128)S(1)} %copy.6), channel_id=1, source_target_pairs={{0,1},{1,2},{2,3},{3,4},{4,5},{5,6},{6,7},{8,9},{9,10},{10,11},{11... | collective-permute-start | bytes 3145736 | tf_op jit(solution)/shard_map/ppermute | solution.py:15
  35.7 28.0 %collective-permute-start.5 = (f32[1,2,2,256,256]{3,4,1,2,0:T(8,128)S(1)}, f32[1,2,2,256,256]{3,4,1,2,0:T(8,128)S(1)}, u32[]{:S(2)}, u32[]{:S(2)}) collective-permute-start(f32[1,2,2,256,256]{3,4,1,2,0:T(8,128)S(1)} %get-tuple-element.7), channel_id=1, source_target_pairs={{0,1},{1,2},{2,3},{3,4},{4,5},{5,6},{6,7},{8,9},{9,10},{10,11},{11... | collective-permute-start | bytes 3145736 | tf_op jit(solution)/shard_map/ppermute | solution.py:15
  40.3 43.9 %collective-permute-start.1 = (f32[1,2,2,256,256]{3,4,1,2,0:T(8,128)S(1)}, f32[1,2,2,256,256]{3,4,1,2,0:T(8,128)}, u32[]{:S(2)}, u32[]{:S(2)}) collective-permute-start(f32[1,2,2,256,256]{3,4,1,2,0:T(8,128)S(1)} %get-tuple-element.8), channel_id=1, source_target_pairs={{0,1},{1,2},{2,3},{3,4},{4,5},{5,6},{6,7},{8,9},{9,10},{10,11},{11... | collective-permute-start | bytes 3145736 | tf_op jit(solution)/shard_map/ppermute | solution.py:15
  64.8 30.1 %collective-permute-start.6 = (f32[1,2,2,256,256]{3,4,1,2,0:T(8,128)}, f32[1,2,2,256,256]{3,4,1,2,0:T(8,128)}, u32[]{:S(2)}, u32[]{:S(2)}) collective-permute-start(f32[1,2,2,256,256]{3,4,1,2,0:T(8,128)} %broadcast_select_fusion), channel_id=1, source_target_pairs={{0,2},{1,3},{2,4},{3,5},{4,6},{5,7},{8,10},{9,11},{10,12},{11,13},... | collective-permute-start | bytes 3145736 | tf_op jit(solution)/shard_map/ppermute | solution.py:15
  85.6 27.0 %collective-permute-start.2 = (f32[1,2,2,256,256]{3,4,1,2,0:T(8,128)S(1)}, f32[1,2,2,256,256]{3,4,1,2,0:T(8,128)}, u32[]{:S(2)}, u32[]{:S(2)}) collective-permute-start(f32[1,2,2,256,256]{3,4,1,2,0:T(8,128)S(1)} %broadcast_select_fusion.4), channel_id=1, source_target_pairs={{0,2},{1,3},{2,4},{3,5},{4,6},{5,7},{8,10},{9,11},{10,12},{11,13},... | collective-permute-start | bytes 3145736 | tf_op jit(solution)/shard_map/ppermute | solution.py:15
  96.3 20.6 %collective-permute-start.7 = (f32[1,2,2,256,256]{3,4,1,2,0:T(8,128)S(1)}, f32[1,2,2,256,256]{3,4,1,2,0:T(8,128)}, u32[]{:S(2)}, u32[]{:S(2)}) collective-permute-start(f32[1,2,2,256,256]{3,4,1,2,0:T(8,128)S(1)} %broadcast_select_fusion.1), channel_id=1, source_target_pairs={{0,8},{8,16},{16,24},{24,0},{1,9},{9,17},{17,25},{25,1},{2,10},{10... | collective-permute-start | bytes 3145736 | tf_op jit(solution)/shard_map/ppermute | solution.py:20
  96.4 17.9 %copy-start.4 = (s32[2]{0:T(128)S(1)}, s32[2]{0:T(128)}, u32[]{:S(2)}) copy-start(s32[2]{0:T(128)} %param.8) | copy-start | bytes 28
  114.0 21.2 %collective-permute-start.3 = (f32[1,2,2,256,256]{3,4,1,2,0:T(8,128)S(1)}, f32[1,2,2,256,256]{3,4,1,2,0:T(8,128)}, u32[]{:S(2)}, u32[]{:S(2)}) collective-permute-start(f32[1,2,2,256,256]{3,4,1,2,0:T(8,128)S(1)} %broadcast_select_fusion.5), channel_id=1, source_target_pairs={{0,8},{8,16},{16,24},{24,0},{1,9},{9,17},{17,25},{25,1},{2,10},{10... | collective-permute-start | bytes 3145736 | tf_op jit(solution)/shard_map/ppermute | solution.py:20
  116.8 4.9 %copy-start.5 = (s32[2]{0:T(128)S(1)}, s32[2]{0:T(128)}, u32[]{:S(2)}) copy-start(s32[2]{0:T(128)} %param.7) | copy-start | bytes 28
  118.2 26.2 %collective-permute-start.8 = (f32[1,2,2,256,256]{3,4,1,2,0:T(8,128)S(1)}, f32[1,2,2,256,256]{3,4,1,2,0:T(8,128)}, u32[]{:S(2)}, u32[]{:S(2)}) collective-permute-start(f32[1,2,2,256,256]{3,4,1,2,0:T(8,128)S(1)} %broadcast_select_fusion.2), channel_id=1, source_target_pairs={{0,16},{8,24},{16,0},{24,8},{1,17},{9,25},{17,1},{25,9},{2,18},{10... | collective-permute-start | bytes 3145736 | tf_op jit(solution)/shard_map/ppermute | solution.py:20
  123.5 13.3 %copy-start.2 = (f32[1,1,2,256,256]{4,3,2,1,0:T(8,128)S(1)}, f32[1,1,2,256,256]{4,3,2,1,0:T(8,128)}, u32[]{:S(2)}) copy-start(f32[1,1,2,256,256]{4,3,2,1,0:T(8,128)} %param.6) | copy-start | bytes 1572868
  135.3 155.0 %collective-permute-start.4 = (f32[1,2,2,256,256]{3,4,1,2,0:T(8,128)S(1)}, f32[1,2,2,256,256]{3,4,1,2,0:T(8,128)}, u32[]{:S(2)}, u32[]{:S(2)}) collective-permute-start(f32[1,2,2,256,256]{3,4,1,2,0:T(8,128)S(1)} %broadcast_select_fusion.6), channel_id=1, source_target_pairs={{0,16},{8,24},{16,0},{24,8},{1,17},{9,25},{17,1},{25,9},{2,18},{10... | collective-permute-start | bytes 3145736 | tf_op jit(solution)/shard_map/ppermute | solution.py:20
  288.0 1.7 copy-start.1
  290.3 1.4 copy-start
Sparse Core Ops, SparseCore 0:
  138.1 149.8 all-reduce.2
where the time goes:
time: 312 us
  waiting for transfers between devices  222 us (71%)
  starting transfers between devices  35.7 us (11%)
  between operations  24.2 us (8%)
  matrix products  14.1 us (5%)
  other arithmetic  10.9 us (3%)
  local copies, waits for them, and re-layouts  4.38 us (1%)
    psum x1, waiting for transfers between devices, spread(): return lax.psum(jnp.where(mine, array, jnp.zeros_like(array)), axis)  142 us
    ppermute x5, waiting for transfers between devices, passed_along(): return lax.ppermute(block, axis, route)  62.2 us
    ppermute x5, starting transfers between devices, passed_along(): return lax.ppermute(block, axis, route)  32.3 us
    ppermute x4, waiting for transfers between devices, shifted(): lax.ppermute(array, axis, [(i, (i + by) % devices) for i in range(devices)])  18 us
    dot_general x8, matrix products, matmul_right(): jnp.einsum('...ij,kj->...ik', left, right, precision=lax.Precision.HIGHEST)  8.18 us
  transfers between devices with their start and end apart: 10, of which 7 were waited for; matrix products, arithmetic and copies ran while one was open for 4% of the time, Pallas kernels for 0%

commit v1 on v0

--- a/solution.py
+++ b/solution.py
@@ -3,10 +3,14 @@
 from jax import lax
 from jax.sharding import PartitionSpec as P
 
+group_run_over_axis = lambda row_data, mesh_name: jnp.sum(
+    lax.all_gather(row_data, mesh_name), axis=0
+)
+
 
 def spread(array, axis, root):
     mine = lax.axis_index(axis) == root
-    return lax.psum(jnp.where(mine, array, jnp.zeros_like(array)), axis)
+    return group_run_over_axis(jnp.where(mine, array, jnp.zeros_like(array)), axis)
 
 
 def passed_along(block, axis, distance):

time: 312 us -> 374 us (1.20)
  the two profiles are of different devices: /device:TPU:0 before, /device:TPU:5 now
where the time goes in v1:
time: 374 us; the launch traced here: 373 us
  waiting for transfers between devices  266 us (71%)
  starting transfers between devices  39.3 us (11%)
  other arithmetic  24.9 us (7%)
  between operations  24.2 us (6%)
  matrix products  15 us (4%)
  local copies, waits for them, and re-layouts  3.92 us (1%)
    ppermute x5, waiting for transfers between devices, passed_along(): return lax.ppermute(block, axis, route)  155 us
    ppermute x4, waiting for transfers between devices, shifted(): lax.ppermute(array, axis, [(i, (i + by) % devices) for i in range(devices)])  82 us
    ppermute x5, starting transfers between devices, passed_along(): return lax.ppermute(block, axis, route)  31.3 us
    all_gather x2, waiting for transfers between devices, lax.all_gather(row_data, mesh_name)  28.3 us
    reduce_sum x2, other arithmetic, jnp.sum(lax.all_gather(row_data, mesh_name), axis=0)  13.9 us
    dot_general x8, matrix products, matmul_right(): jnp.einsum('...ij,kj->...ik', left, right, precision=lax.Precision.HIGHEST)  8.41 us
    ppermute x4, starting transfers between devices, shifted(): lax.ppermute(array, axis, [(i, (i + by) % devices) for i in range(devices)])  7.97 us
  transfers between devices with their start and end apart: 11, of which 9 were waited for; matrix products, arithmetic and copies ran while one was open for 5% of the time, Pallas kernels for 0%

profile of v1, /device:TPU:5, one launch (start us, length us, event | category | flops | bytes accessed | tf_op | source)
XLA Modules:
  0.0 373.4 jit_solution(8919216343084254180)
XLA Ops:
  6.5 1.3 fusion.18
  9.2 2.1 broadcast_select_fusion.8
  12.5 3.1 collective-permute-start
  20.1 28.5 %collective-permute-done = f32[1,2,2,256,256]{3,4,1,2,0:T(8,128)} collective-permute-done((f32[1,2,2,256,256]{3,4,1,2,0:T(8,128)S(1)}, f32[1,2,2,256,256]{3,4,1,2,0:T(8,128)}, u32[]{:S(2)}, u32[]{:S(2)}) %collective-permute-start) | collective-permute-done | bytes 1048608 | tf_op jit(solution)/shard_map/ppermute | solution.py:19
  48.9 5.1 %collective-permute-start.5 = (f32[1,2,2,256,256]{3,4,1,2,0:T(8,128)S(1)}, f32[1,2,2,256,256]{3,4,1,2,0:T(8,128)}, u32[]{:S(2)}, u32[]{:S(2)}) collective-permute-start(f32[1,2,2,256,256]{3,4,1,2,0:T(8,128)S(1)} %get-tuple-element.5), channel_id=1, source_target_pairs={{0,1},{1,2},{2,3},{3,4},{4,5},{5,6},{6,7},{8,9},{9,10},{10,11},{11... | collective-permute-start | bytes 3145736 | tf_op jit(solution)/shard_map/ppermute | solution.py:19
  54.0 1.9 collective-permute-start.1
  57.3 38.3 %collective-permute-done.5 = f32[1,2,2,256,256]{3,4,1,2,0:T(8,128)} collective-permute-done((f32[1,2,2,256,256]{3,4,1,2,0:T(8,128)S(1)}, f32[1,2,2,256,256]{3,4,1,2,0:T(8,128)}, u32[]{:S(2)}, u32[]{:S(2)}) %collective-permute-start.5) | collective-permute-done | bytes 1048608 | tf_op jit(solution)/shard_map/ppermute | solution.py:19
  95.8 4.3 %collective-permute-start.6 = (f32[1,2,2,256,256]{3,4,1,2,0:T(8,128)S(1)}, f32[1,2,2,256,256]{3,4,1,2,0:T(8,128)}, u32[]{:S(2)}, u32[]{:S(2)}) collective-permute-start(f32[1,2,2,256,256]{3,4,1,2,0:T(8,128)S(1)} %broadcast_select_fusion), channel_id=1, source_target_pairs={{0,2},{1,3},{2,4},{3,5},{4,6},{5,7},{8,10},{9,11},{10,12},{11,13},... | collective-permute-start | bytes 3145736 | tf_op jit(solution)/shard_map/ppermute | solution.py:19
  100.1 37.4 %collective-permute-done.1 = f32[1,2,2,256,256]{3,4,1,2,0:T(8,128)} collective-permute-done((f32[1,2,2,256,256]{3,4,1,2,0:T(8,128)S(1)}, f32[1,2,2,256,256]{3,4,1,2,0:T(8,128)}, u32[]{:S(2)}, u32[]{:S(2)}) %collective-permute-start.1) | collective-permute-done | bytes 1048608 | tf_op jit(solution)/shard_map/ppermute | solution.py:19
  137.5 1.4 broadcast_select_fusion.4
  138.9 16.8 %collective-permute-start.2 = (f32[1,2,2,256,256]{3,4,1,2,0:T(8,128)S(1)}, f32[1,2,2,256,256]{3,4,1,2,0:T(8,128)}, u32[]{:S(2)}, u32[]{:S(2)}) collective-permute-start(f32[1,2,2,256,256]{3,4,1,2,0:T(8,128)S(1)} %broadcast_select_fusion.4), channel_id=1, source_target_pairs={{0,2},{1,3},{2,4},{3,5},{4,6},{5,7},{8,10},{9,11},{10,12},{11,13},... | collective-permute-start | bytes 3145736 | tf_op jit(solution)/shard_map/ppermute | solution.py:19
  155.6 26.8 %collective-permute-done.6 = f32[1,2,2,256,256]{3,4,1,2,0:T(8,128)} collective-permute-done((f32[1,2,2,256,256]{3,4,1,2,0:T(8,128)S(1)}, f32[1,2,2,256,256]{3,4,1,2,0:T(8,128)}, u32[]{:S(2)}, u32[]{:S(2)}) %collective-permute-start.6) | collective-permute-done | bytes 1048608 | tf_op jit(solution)/shard_map/ppermute | solution.py:19
  182.4 1.4 broadcast_select_fusion.1
  183.8 4.0 %collective-permute-start.7 = (f32[1,2,2,256,256]{3,4,1,2,0:T(8,128)S(1)}, f32[1,2,2,256,256]{3,4,1,2,0:T(8,128)}, u32[]{:S(2)}, u32[]{:S(2)}) collective-permute-start(f32[1,2,2,256,256]{3,4,1,2,0:T(8,128)S(1)} %broadcast_select_fusion.1), channel_id=1, source_target_pairs={{0,8},{8,16},{16,24},{24,0},{1,9},{9,17},{17,25},{25,1},{2,10},{10... | collective-permute-start | bytes 3145736 | tf_op jit(solution)/shard_map/ppermute | solution.py:24
  187.8 24.0 %collective-permute-done.2 = f32[1,2,2,256,256]{3,4,1,2,0:T(8,128)} collective-permute-done((f32[1,2,2,256,256]{3,4,1,2,0:T(8,128)S(1)}, f32[1,2,2,256,256]{3,4,1,2,0:T(8,128)}, u32[]{:S(2)}, u32[]{:S(2)}) %collective-permute-start.2) | collective-permute-done | bytes 1048608 | tf_op jit(solution)/shard_map/ppermute | solution.py:19
  211.8 1.4 broadcast_select_fusion.5
  213.2 3.6 collective-permute-start.3
  221.2 1.4 broadcast_select_fusion.2
  223.0 15.5 %collective-permute-done.3 = f32[1,2,2,256,256]{3,4,1,2,0:T(8,128)} collective-permute-done((f32[1,2,2,256,256]{3,4,1,2,0:T(8,128)S(1)}, f32[1,2,2,256,256]{3,4,1,2,0:T(8,128)}, u32[]{:S(2)}, u32[]{:S(2)}) %collective-permute-start.3) | collective-permute-done | bytes 1048608 | tf_op jit(solution)/shard_map/ppermute | solution.py:24
  238.8 32.9 %collective-permute-done.8 = f32[1,2,2,256,256]{3,4,1,2,0:T(8,128)} collective-permute-done((f32[1,2,2,256,256]{3,4,1,2,0:T(8,128)S(1)}, f32[1,2,2,256,256]{3,4,1,2,0:T(8,128)}, u32[]{:S(2)}, u32[]{:S(2)}) %collective-permute-start.8) | collective-permute-done | bytes 1048608 | tf_op jit(solution)/shard_map/ppermute | solution.py:24
  271.7 1.4 broadcast_select_fusion.3
  273.0 33.6 %collective-permute-done.4 = f32[1,2,2,256,256]{3,4,1,2,0:T(8,128)} collective-permute-done((f32[1,2,2,256,256]{3,4,1,2,0:T(8,128)S(1)}, f32[1,2,2,256,256]{3,4,1,2,0:T(8,128)}, u32[]{:S(2)}, u32[]{:S(2)}) %collective-permute-start.4) | collective-permute-done | bytes 1048608 | tf_op jit(solution)/shard_map/ppermute | solution.py:24
  306.7 1.4 broadcast_select_fusion.7
  308.1 7.0 %reduce_sum.19 = f32[2,256,256]{2,1,0:T(8,128)S(1)} reduce(f32[32,1,2,256,256]{4,3,2,1,0:T(8,128)} %all-gather.7.cloned.1.call-done, f32[]{:T(128)} %constant.155.clone.1), dimensions={0,1}, to_apply=%region_1.2 | reduce | flops 4063232 | bytes 17301508 | tf_op jit(solution)/shard_map/reduce_sum | solution.py:6
  315.1 1.4 fusion.12
  316.5 1.4 fusion.13
  317.9 28.3 %all-gather.5.cloned.1.call-done = f32[32,1,2,256,256]{4,3,2,1,0:T(8,128)} async-done(((f32[1,1,2,256,256]{4,3,2,1,0:T(8,128)}), f32[32,1,2,256,256]{4,3,2,1,0:T(8,128)}) %all-gather.5.cloned.1.call-update) | async-done | bytes 16777232 | tf_op jit(solution)/shard_map/all_gather | solution.py:7
  346.2 6.9 %reduce_sum.18 = f32[2,256,256]{2,1,0:T(8,128)S(1)} reduce(f32[32,1,2,256,256]{4,3,2,1,0:T(8,128)} %all-gather.5.cloned.1.call-done, f32[]{:T(128)} %constant.155.clone.1), dimensions={0,1}, to_apply=%region_0.1 | reduce | flops 4063232 | bytes 17301508 | tf_op jit(solution)/shard_map/reduce_sum | solution.py:6
  357.7 1.0 fusion
  360.4 1.2 fusion.14
  363.3 1.0 fusion.4
  365.5 1.0 copy.27
  (42 shorter events, 12.2 us)
Async XLA Ops:
  6.5 5.6 %copy-start.5 = (f32[1,2,2,256,256]{4,3,2,1,0:T(8,128)S(1)}, f32[1,2,2,256,256]{4,3,2,1,0:T(8,128)}, u32[]{:S(2)}) copy-start(f32[1,2,2,256,256]{4,3,2,1,0:T(8,128)} %param.5) | copy-start | bytes 3145732
  6.5 301.5 %all-gather.7.cloned.1.call-start = ((), (), s32[]{:S(2)}) async-start(), calls=%async_computation.1 | async-start | bytes 17301504 | tf_op jit(solution)/shard_map/all_gather | solution.py:7
  9.2 6.4 %copy-start.6 = (s32[2]{0:T(128)S(1)}, s32[2]{0:T(128)}, u32[]{:S(2)}) copy-start(s32[2]{0:T(128)} %param.9) | copy-start | bytes 28
  11.3 334.8 %all-gather.5.cloned.1.call-start = ((), (), s32[]{:S(2)}) async-start(), calls=%async_computation | async-start | bytes 17301504 | tf_op jit(solution)/shard_map/all_gather | solution.py:7
  12.5 36.2 %collective-permute-start = (f32[1,2,2,256,256]{3,4,1,2,0:T(8,128)S(1)}, f32[1,2,2,256,256]{3,4,1,2,0:T(8,128)}, u32[]{:S(2)}, u32[]{:S(2)}) collective-permute-start(f32[1,2,2,256,256]{3,4,1,2,0:T(8,128)S(1)} %copy.17), channel_id=1, source_target_pairs={{0,1},{1,2},{2,3},{3,4},{4,5},{5,6},{6,7},{8,9},{9,10},{10,11},{11... | collective-permute-start | bytes 3145736 | tf_op jit(solution)/shard_map/ppermute | solution.py:19
  48.9 46.7 %collective-permute-start.5 = (f32[1,2,2,256,256]{3,4,1,2,0:T(8,128)S(1)}, f32[1,2,2,256,256]{3,4,1,2,0:T(8,128)}, u32[]{:S(2)}, u32[]{:S(2)}) collective-permute-start(f32[1,2,2,256,256]{3,4,1,2,0:T(8,128)S(1)} %get-tuple-element.5), channel_id=1, source_target_pairs={{0,1},{1,2},{2,3},{3,4},{4,5},{5,6},{6,7},{8,9},{9,10},{10,11},{11... | collective-permute-start | bytes 3145736 | tf_op jit(solution)/shard_map/ppermute | solution.py:19
  54.0 83.5 %collective-permute-start.1 = (f32[1,2,2,256,256]{3,4,1,2,0:T(8,128)S(1)}, f32[1,2,2,256,256]{3,4,1,2,0:T(8,128)}, u32[]{:S(2)}, u32[]{:S(2)}) collective-permute-start(f32[1,2,2,256,256]{3,4,1,2,0:T(8,128)S(1)} %get-tuple-element.6), channel_id=1, source_target_pairs={{0,1},{1,2},{2,3},{3,4},{4,5},{5,6},{6,7},{8,9},{9,10},{10,11},{11... | collective-permute-start | bytes 3145736 | tf_op jit(solution)/shard_map/ppermute | solution.py:19
  95.8 86.7 %collective-permute-start.6 = (f32[1,2,2,256,256]{3,4,1,2,0:T(8,128)S(1)}, f32[1,2,2,256,256]{3,4,1,2,0:T(8,128)}, u32[]{:S(2)}, u32[]{:S(2)}) collective-permute-start(f32[1,2,2,256,256]{3,4,1,2,0:T(8,128)S(1)} %broadcast_select_fusion), channel_id=1, source_target_pairs={{0,2},{1,3},{2,4},{3,5},{4,6},{5,7},{8,10},{9,11},{10,12},{11,13},... | collective-permute-start | bytes 3145736 | tf_op jit(solution)/shard_map/ppermute | solution.py:19
  138.9 48.9 %copy-start.1 = (f32[1,2,2,256,256]{3,4,1,2,0:T(8,128)}, f32[1,2,2,256,256]{3,4,1,2,0:T(8,128)S(1)}, u32[]{:S(2)}) copy-start(f32[1,2,2,256,256]{3,4,1,2,0:T(8,128)S(1)} %broadcast_select_fusion.4) | copy-start | bytes 3145732
  138.9 72.9 %collective-permute-start.2 = (f32[1,2,2,256,256]{3,4,1,2,0:T(8,128)S(1)}, f32[1,2,2,256,256]{3,4,1,2,0:T(8,128)}, u32[]{:S(2)}, u32[]{:S(2)}) collective-permute-start(f32[1,2,2,256,256]{3,4,1,2,0:T(8,128)S(1)} %broadcast_select_fusion.4), channel_id=1, source_target_pairs={{0,2},{1,3},{2,4},{3,5},{4,6},{5,7},{8,10},{9,11},{10,12},{11,13},... | collective-permute-start | bytes 3145736 | tf_op jit(solution)/shard_map/ppermute | solution.py:19
  183.8 32.9 %copy-start.7 = (s32[2]{0:T(128)S(1)}, s32[2]{0:T(128)}, u32[]{:S(2)}) copy-start(s32[2]{0:T(128)} %param.8) | copy-start | bytes 28
  183.8 37.4 %collective-permute-start.7 = (f32[1,2,2,256,256]{3,4,1,2,0:T(8,128)S(1)}, f32[1,2,2,256,256]{3,4,1,2,0:T(8,128)}, u32[]{:S(2)}, u32[]{:S(2)}) collective-permute-start(f32[1,2,2,256,256]{3,4,1,2,0:T(8,128)S(1)} %broadcast_select_fusion.1), channel_id=1, source_target_pairs={{0,8},{8,16},{16,24},{24,0},{1,9},{9,17},{17,25},{25,1},{2,10},{10... | collective-permute-start | bytes 3145736 | tf_op jit(solution)/shard_map/ppermute | solution.py:24
  213.2 25.3 %collective-permute-start.3 = (f32[1,2,2,256,256]{3,4,1,2,0:T(8,128)S(1)}, f32[1,2,2,256,256]{3,4,1,2,0:T(8,128)}, u32[]{:S(2)}, u32[]{:S(2)}) collective-permute-start(f32[1,2,2,256,256]{3,4,1,2,0:T(8,128)S(1)} %broadcast_select_fusion.5), channel_id=1, source_target_pairs={{0,8},{8,16},{16,24},{24,0},{1,9},{9,17},{17,25},{25,1},{2,10},{10... | collective-permute-start | bytes 3145736 | tf_op jit(solution)/shard_map/ppermute | solution.py:24
  222.6 16.1 %copy-start = (f32[1,2,2,256,256]{3,4,1,2,0:T(8,128)}, f32[1,2,2,256,256]{3,4,1,2,0:T(8,128)S(1)}, u32[]{:S(2)}) copy-start(f32[1,2,2,256,256]{3,4,1,2,0:T(8,128)S(1)} %broadcast_select_fusion.2) | copy-start | bytes 3145732
  222.6 49.0 %collective-permute-start.8 = (f32[1,2,2,256,256]{3,4,1,2,0:T(8,128)S(1)}, f32[1,2,2,256,256]{3,4,1,2,0:T(8,128)}, u32[]{:S(2)}, u32[]{:S(2)}) collective-permute-start(f32[1,2,2,256,256]{3,4,1,2,0:T(8,128)S(1)} %broadcast_select_fusion.2), channel_id=1, source_target_pairs={{0,16},{8,24},{16,0},{24,8},{1,17},{9,25},{17,1},{25,9},{2,18},{10... | collective-permute-start | bytes 3145736 | tf_op jit(solution)/shard_map/ppermute | solution.py:24
  238.6 34.4 %copy-start.2 = (f32[1,2,2,256,256]{3,4,1,2,0:T(8,128)}, f32[1,2,2,256,256]{3,4,1,2,0:T(8,128)S(1)}, u32[]{:S(2)}) copy-start(f32[1,2,2,256,256]{3,4,1,2,0:T(8,128)S(1)} %broadcast_select_fusion.6) | copy-start | bytes 3145732
  238.6 68.1 %collective-permute-start.4 = (f32[1,2,2,256,256]{3,4,1,2,0:T(8,128)S(1)}, f32[1,2,2,256,256]{3,4,1,2,0:T(8,128)}, u32[]{:S(2)}, u32[]{:S(2)}) collective-permute-start(f32[1,2,2,256,256]{3,4,1,2,0:T(8,128)S(1)} %broadcast_select_fusion.6), channel_id=1, source_target_pairs={{0,16},{8,24},{16,0},{24,8},{1,17},{9,25},{17,1},{25,9},{2,18},{10... | collective-permute-start | bytes 3145736 | tf_op jit(solution)/shard_map/ppermute | solution.py:24
  353.1 1.3 copy-start.4
  353.7 2.3 copy-start.3
Sparse Core Ops, SparseCore 0:
  11.5 177.2 all-gather.6
  191.9 154.2 all-gather.4
